TPU v7x, 32 devices: a whole 2x2x4 slice. The times are simulated.
32 devices in a mesh: row: 2 (over x), col: 4 (over y, core), layer: 4 (over z).
Axes of the slice: x: 2, y: 2, z: 4, core: 2. Of those that a mesh axis runs over, the one named last changes fastest.
Arguments:
- flow_matrix: float32 [2048, 2048], P('row', ('layer', 'col')), may hold values from 0.0009 to 310, as said below
- regularizer: float32 [2048, 2048], P(('layer', 'row'), 'col'), may hold values from 0.001 to 1
- pattern: int32 [8, 8], replicated, may hold values from 0 to 1, as said below
Outputs:
- inflated: float32 [2048, 2048], P(('row', 'layer'), 'col')
Inputs may be any that keep to these rules, and one draw needn't show every extreme that they name: `flow_matrix`: entries are positive. `pattern`: each entry is 0 or 1; every diagonal entry is 1.
All inputs are finite; a program needn't handle non-finite values.
Results may differ from a plain program's by a relative error of at most 0.000098.
Values sent between devices are 32-bit elements; how exact they have to be, the bound alone decides.
No kernel may reach another device: no remote copies, remote signals or barrier semaphores. Data moves between devices by JAX's collectives and lax.ppermute only.
A program may use at most 64 MiB of HBM per device.

v0:
```python
import jax
import jax.numpy as jnp
from jax import lax
from jax.sharding import PartitionSpec as P

TILE = 256


def keep_tiles(values, pattern, row_start, col_start):
    tile_count = pattern.shape[0]
    row_tile = (row_start + lax.iota(jnp.int32, values.shape[0])) // TILE
    col_tile = (col_start + lax.iota(jnp.int32, values.shape[1])) // TILE
    tile_ids = lax.iota(jnp.int32, tile_count)
    row_pick = (row_tile[:, None] == tile_ids[None, :]).astype(jnp.float32)
    col_pick = (col_tile[:, None] == tile_ids[None, :]).astype(jnp.float32)
    pattern_rows = jnp.dot(
        row_pick,
        pattern.astype(jnp.float32),
        precision=lax.Precision.HIGHEST,
        preferred_element_type=jnp.float32,
    )
    chosen = jnp.dot(
        pattern_rows,
        col_pick.T,
        precision=lax.Precision.HIGHEST,
        preferred_element_type=jnp.float32,
    )
    return values * chosen


def shards(flow_matrix, regularizer, pattern):
    order_total = flow_matrix.shape[0] * lax.axis_size("row")
    left_whole = lax.all_gather(flow_matrix, "col", axis=1, tiled=True)
    partial_value = jnp.dot(
        left_whole,
        lax.all_gather(regularizer, "row", axis=0, tiled=True),
        precision=lax.Precision.HIGHEST,
        preferred_element_type=jnp.float32,
    )
    own_count = partial_value.shape[0] // lax.axis_size("layer")
    col_start = lax.axis_index("col") * partial_value.shape[1]
    expanded = lax.psum_scatter(partial_value, "layer", scatter_dimension=0, tiled=True)
    row_start = lax.axis_index("row") * partial_value.shape[0] + lax.axis_index("layer") * own_count
    pruned = keep_tiles(expanded, pattern, row_start, col_start)
    squared = pruned * pruned
    totals = lax.psum(jnp.sum(squared, axis=0), ("row", "layer"))
    inflated = squared / totals[None, :] * order_total
    return inflated


def solution(mesh):
    return jax.shard_map(
        shards,
        mesh=mesh,
        in_specs=(P("row", ("layer", "col")), P(("layer", "row"), "col"), P()),
        out_specs=P(("row", "layer"), "col"),
        check_vma=False,
    )
```

profile of v0, /device:TPU:0, one launch (start us, length us, event | category | flops | bytes accessed | tf_op | source)
XLA Modules:
  0.0 136.4 jit_solution(12964221598717887879)
XLA Ops:
  6.5 0.0 all-gather.5.cloned.1.call-start
  6.5 0.7 all-gather.5.cloned.1.call-update
  7.3 0.0 all-gather.3.cloned.1.call-start
  7.3 0.7 all-gather.3.cloned.1.call-update
  8.0 0.0 reduce-scatter.2.cloned.1.call-start
  8.1 24.9 %all-gather.5.cloned.1.call-done = f32[512,512]{1,0:T(8,128)} async-done(((f32[256,512]{1,0:T(8,128)}), f32[512,512]{1,0:T(8,128)}) %all-gather.5.cloned.1.call-update) | async-done | bytes 1048592 | tf_op jit(solution)/shard_map/all_gather | solution.py:36
  32.9 24.4 %all-gather.3.cloned.1.call-done = f32[1024,512]{1,0:T(8,128)} async-done(((f32[1024,128]{1,0:T(8,128)}), f32[1024,512]{1,0:T(8,128)}) %all-gather.3.cloned.1.call-update) | async-done | bytes 2097168 | tf_op jit(solution)/shard_map/all_gather | solution.py:33
  57.3 6.6 %fusion.9 = f32[1024,512]{1,0:T(8,128)} fusion(f32[1024,512]{1,0:T(8,128)} %all-gather.3.cloned.1.call-done, f32[512,512]{1,0:T(8,128)} %all-gather.5.cloned.1.call-done), kind=kOutput, calls=%fused_computation.23 | convolution fusion | flops 3221225472 | bytes 5242880 | tf_op jit(solution)/shard_map/dot_general | solution.py:34
  63.9 0.0 copy-start
  63.9 0.0 reduce-scatter.2.cloned.1.call-update
  64.0 0.6 copy-done
  64.6 0.3 fusion.2
  64.9 42.9 %reduce-scatter.2.cloned.1.call-done = f32[256,512]{1,0:T(8,128)} async-done(((f32[1024,512]{1,0:T(8,128)}), f32[256,512]{1,0:T(8,128)}) %reduce-scatter.2.cloned.1.call-update) | async-done | bytes 524304 | tf_op jit(solution)/shard_map/reduce_scatter | solution.py:42
  107.8 1.6 %fusion.8 = (f32[512]{0:T(512)S(1)}, f32[256,512]{1,0:T(8,128)S(1)}) fusion(f32[256,512]{1,0:T(8,128)} %reduce-scatter.2.cloned.1.call-done, f32[256,8]{1,0:T(8,128)S(1)} %fusion.2, s32[512]{0:T(512)S(1)} %add_select_fusion), kind=kOutput, calls=%fused_computation.22 | convolution fusion | flops 12979712 | bytes 1060864 | tf_op jit(solution)/shard_map/dot_general | solution.py:22
  109.3 19.7 %psum.7 = f32[512]{0:T(512)S(1)} all-reduce(f32[512]{0:T(512)S(1)} %get-tuple-element.5), channel_id=1, replica_groups=mesh['row'=2,'col'=4,'layer'=4] {'row','layer'}, use_global_device_ids=true, to_apply=%region_2.3 | all-reduce | flops 512 | bytes 4096 | tf_op jit(solution)/shard_map/psum | solution.py:46
  129.0 0.9 divide_multiply_fusion
  (2 shorter events, 0.0 us)
Async XLA Ops:
  6.5 26.4 %all-gather.5.cloned.1.call-start = ((), (), s32[]{:S(2)}) async-start(), calls=%async_computation.2 | async-start | bytes 1572864 | tf_op jit(solution)/shard_map/all_gather | solution.py:36
  7.3 50.1 %all-gather.3.cloned.1.call-start = ((), (), s32[]{:S(2)}) async-start(), calls=%async_computation.1 | async-start | bytes 2621440 | tf_op jit(solution)/shard_map/all_gather | solution.py:33
  8.0 99.8 %reduce-scatter.2.cloned.1.call-start = ((), (), s32[]{:S(2)}) async-start(), calls=%async_computation.3 | async-start | bytes 2621440 | tf_op jit(solution)/shard_map/reduce_scatter | solution.py:42
  63.9 0.7 copy-start
Sparse Core Ops, SparseCore 0:
  8.9 23.9 all-gather.4
  34.5 22.8 all-gather.2
  64.1 43.6 reduce-scatter.1
where the time goes:
time: 137 us; the launch traced here: 136 us
  waiting for transfers between devices  93.5 us (68%)
  blocking collectives  19.7 us (14%)
  between operations  13.1 us (10%)
  matrix products  8.44 us (6%)
    reduce_scatter x1, waiting for transfers between devices, shards(): lax.psum_scatter(partial_value, 'layer', scatter_dimension=0, tiled=True)  42.9 us
    all_gather x1, waiting for transfers between devices, shards(): lax.all_gather(regularizer, 'row', axis=0, tiled=True)  24.9 us
    all_gather x1, waiting for transfers between devices, shards(): left_whole = lax.all_gather(flow_matrix, 'col', axis=1, tiled=True)  24.4 us
    psum x1, blocking collectives, shards(): totals = lax.psum(jnp.sum(squared, axis=0), ('row', 'layer'))  19.7 us
    dot_general x1, matrix products, shards(): jnp.dot(left_whole, lax.all_gather(regularizer, 'row', axis=0, tiled=True...  6.63 us
  transfers between devices with their start and end apart: 3, of which 3 were waited for; matrix products, arithmetic and copies ran while one was open for 0% of the time, Pallas kernels for 0%

commit v1 on v0

--- a/solution.py
+++ b/solution.py
@@ -43,7 +43,7 @@
     row_start = lax.axis_index("row") * partial_value.shape[0] + lax.axis_index("layer") * own_count
     pruned = keep_tiles(expanded, pattern, row_start, col_start)
     squared = pruned * pruned
-    totals = lax.psum(jnp.sum(squared, axis=0), ("row", "layer"))
+    totals = jnp.sum(lax.all_gather(jnp.sum(squared, axis=0), ("row", "layer")), axis=0)
     inflated = squared / totals[None, :] * order_total
     return inflated
 

time: 137 us -> 144 us (1.051)
  blocking collectives: 19.7 us -> 27 us
    all_gather x0 -> x1, blocking collectives: none -> 27 us  [shards(): lax.all_gather(jnp.sum(squared, axis=0), ('row', 'layer'))]
    psum x1 -> x0, blocking collectives: 19.7 us -> none  [shards(): totals = lax.psum(jnp.sum(squared, axis=0), ('row', 'layer'))]
where the time goes in v1:
time: 144 us
  waiting for transfers between devices  93.5 us (65%)
  blocking collectives  27 us (19%)
  between operations  13.1 us (9%)
  matrix products  8.44 us (6%)
    reduce_scatter x1, waiting for transfers between devices, shards(): lax.psum_scatter(partial_value, 'layer', scatter_dimension=0, tiled=True)  42.9 us
    all_gather x1, blocking collectives, shards(): lax.all_gather(jnp.sum(squared, axis=0), ('row', 'layer'))  27 us
    all_gather x1, waiting for transfers between devices, shards(): lax.all_gather(regularizer, 'row', axis=0, tiled=True)  24.9 us
    all_gather x1, waiting for transfers between devices, shards(): left_whole = lax.all_gather(flow_matrix, 'col', axis=1, tiled=True)  24.4 us
    dot_general x1, matrix products, shards(): jnp.dot(left_whole, lax.all_gather(regularizer, 'row', axis=0, tiled=True...  6.63 us
  transfers between devices with their start and end apart: 3, of which 3 were waited for; matrix products, arithmetic and copies ran while one was open for 0% of the time, Pallas kernels for 0%

profile of v1, /device:TPU:0, one launch (start us, length us, event | category | flops | bytes accessed | tf_op | source)
XLA Modules:
  0.0 143.8 jit_solution(2477804963000191579)
XLA Ops:
  6.5 0.0 all-gather.7.cloned.1.call-start
  6.5 0.7 all-gather.7.cloned.1.call-update
  7.3 0.0 all-gather.5.cloned.1.call-start
  7.3 0.7 all-gather.5.cloned.1.call-update
  8.0 0.0 reduce-scatter.2.cloned.1.call-start
  8.1 24.9 %all-gather.7.cloned.1.call-done = f32[512,512]{1,0:T(8,128)} async-done(((f32[256,512]{1,0:T(8,128)}), f32[512,512]{1,0:T(8,128)}) %all-gather.7.cloned.1.call-update) | async-done | bytes 1048592 | tf_op jit(solution)/shard_map/all_gather | solution.py:36
  32.9 24.4 %all-gather.5.cloned.1.call-done = f32[1024,512]{1,0:T(8,128)} async-done(((f32[1024,128]{1,0:T(8,128)}), f32[1024,512]{1,0:T(8,128)}) %all-gather.5.cloned.1.call-update) | async-done | bytes 2097168 | tf_op jit(solution)/shard_map/all_gather | solution.py:33
  57.3 6.6 %fusion.9 = f32[1024,512]{1,0:T(8,128)} fusion(f32[1024,512]{1,0:T(8,128)} %all-gather.5.cloned.1.call-done, f32[512,512]{1,0:T(8,128)} %all-gather.7.cloned.1.call-done), kind=kOutput, calls=%fused_computation.23 | convolution fusion | flops 3221225472 | bytes 5242880 | tf_op jit(solution)/shard_map/dot_general | solution.py:34
  63.9 0.0 copy-start
  63.9 0.0 reduce-scatter.2.cloned.1.call-update
  64.0 0.6 copy-done
  64.6 0.3 fusion.2
  64.9 42.9 %reduce-scatter.2.cloned.1.call-done = f32[256,512]{1,0:T(8,128)} async-done(((f32[1024,512]{1,0:T(8,128)}), f32[256,512]{1,0:T(8,128)}) %reduce-scatter.2.cloned.1.call-update) | async-done | bytes 524304 | tf_op jit(solution)/shard_map/reduce_scatter | solution.py:42
  107.8 1.6 %fusion.8 = (f32[512]{0:T(512)S(1)}, f32[256,512]{1,0:T(8,128)S(1)}) fusion(f32[256,512]{1,0:T(8,128)} %reduce-scatter.2.cloned.1.call-done, f32[256,8]{1,0:T(8,128)S(1)} %fusion.2, s32[512]{0:T(512)S(1)} %add_select_fusion), kind=kOutput, calls=%fused_computation.22 | convolution fusion | flops 12979712 | bytes 1060864 | tf_op jit(solution)/shard_map/dot_general | solution.py:22
  109.3 27.0 %all-gather.1 = f32[8,1,512]{2,1,0:T(1,128)S(1)} all-gather(f32[1,1,512]{2,1,0:T(1,128)S(1)} %bitcast.4), channel_id=2, replica_groups=mesh['row'=2,'col'=4,'layer'=4] {'row','layer'}, dimensions={0}, use_global_device_ids=true | all-gather | bytes 18432 | tf_op jit(solution)/shard_map/all_gather | solution.py:46
  136.4 0.9 divide_multiply_fusion
  (3 shorter events, 0.0 us)
Async XLA Ops:
  6.5 26.4 %all-gather.7.cloned.1.call-start = ((), (), s32[]{:S(2)}) async-start(), calls=%async_computation.2 | async-start | bytes 1572864 | tf_op jit(solution)/shard_map/all_gather | solution.py:36
  7.3 50.1 %all-gather.5.cloned.1.call-start = ((), (), s32[]{:S(2)}) async-start(), calls=%async_computation.1 | async-start | bytes 2621440 | tf_op jit(solution)/shard_map/all_gather | solution.py:33
  8.0 99.8 %reduce-scatter.2.cloned.1.call-start = ((), (), s32[]{:S(2)}) async-start(), calls=%async_computation.3 | async-start | bytes 2621440 | tf_op jit(solution)/shard_map/reduce_scatter | solution.py:42
  63.9 0.7 copy-start
Sparse Core Ops, SparseCore 0:
  8.9 23.9 all-gather.6
  34.5 22.8 all-gather.4
  64.1 43.6 reduce-scatter.1

commit v2 on v0

--- a/solution.py
+++ b/solution.py
@@ -30,7 +30,12 @@
 
 def shards(flow_matrix, regularizer, pattern):
     order_total = flow_matrix.shape[0] * lax.axis_size("row")
-    left_whole = lax.all_gather(flow_matrix, "col", axis=1, tiled=True)
+    ring = [flow_matrix]
+    for hop in range(3):
+        ring.append(lax.ppermute(ring[-1], "col", [(dev, (dev + 1) % 4) for dev in range(4)]))
+    left_whole = jnp.roll(
+        jnp.concatenate(ring[::-1], axis=1), (lax.axis_index("col") + 1) * ring[0].shape[1], axis=1
+    )
     partial_value = jnp.dot(
         left_whole,
         lax.all_gather(regularizer, "row", axis=0, tiled=True),

time: 137 us -> 129 us (0.942)
  waiting for transfers between devices: 93.5 us -> 76.8 us
  local copies, waits for them, and re-layouts: 0.62 us -> 8.06 us
    ppermute x0 -> x3, waiting for transfers between devices: none -> 26.2 us  [shards(): lax.ppermute(ring[-1], 'col', [(dev, (dev + 1) % 4) for dev in range(4)])]
    all_gather x1 -> x0, waiting for transfers between devices: 24.4 us -> none  [shards(): left_whole = lax.all_gather(flow_matrix, 'col', axis=1, tiled=True)]
    all_gather x1, waiting for transfers between devices: 24.9 us -> 7.08 us  [shards(): lax.all_gather(regularizer, 'row', axis=0, tiled=True)]
    unnamed x2 -> x11, local copies, waits for them, and re-layouts: 0.62 us -> 7.19 us
    unnamed x3 -> x2, waiting for transfers between devices: 1.42 us -> 0.03 us
  transfers between devices with their start and end apart: 3 -> 5, of which waited for: 3 -> 5; matrix products, arithmetic and copies ran while one was open for 0% -> 6% of each run, Pallas kernels for 0% -> 0%
where the time goes in v2:
time: 129 us
  waiting for transfers between devices  76.8 us (60%)
  blocking collectives  19.7 us (15%)
  between operations  13.5 us (10%)
  matrix products  8.41 us (7%)
  local copies, waits for them, and re-layouts  8.06 us (6%)
  other arithmetic  1.97 us (2%)
    reduce_scatter x1, waiting for transfers between devices, shards(): lax.psum_scatter(partial_value, 'layer', scatter_dimension=0, tiled=True)  43.5 us
    ppermute x3, waiting for transfers between devices, shards(): lax.ppermute(ring[-1], 'col', [(dev, (dev + 1) % 4) for dev in range(4)])  26.2 us
    psum x1, blocking collectives, shards(): totals = lax.psum(jnp.sum(squared, axis=0), ('row', 'layer'))  19.7 us
    unnamed x11, local copies, waits for them, and re-layouts  7.19 us
    all_gather x1, waiting for transfers between devices, shards(): lax.all_gather(regularizer, 'row', axis=0, tiled=True)  7.08 us
    dot_general x1, matrix products, shards(): jnp.dot(left_whole, lax.all_gather(regularizer, 'row', axis=0, tiled=True...  6.6 us
  transfers between devices with their start and end apart: 5, of which 5 were waited for; matrix products, arithmetic and copies ran while one was open for 6% of the time, Pallas kernels for 0%

profile of v2, /device:TPU:0, one launch (start us, length us, event | category | flops | bytes accessed | tf_op | source)
XLA Modules:
  0.0 128.9 jit_solution(17380092334435893907)
XLA Ops:
  6.5 0.0 copy-start
  6.5 0.0 all-gather.2.cloned.1.call-start
  6.5 0.5 collective-permute-start
  7.0 9.1 %collective-permute-done = f32[1024,128]{1,0:T(8,128)S(1)} collective-permute-done((f32[1024,128]{1,0:T(8,128)}, f32[1024,128]{1,0:T(8,128)S(1)}, u32[]{:S(2)}, u32[]{:S(2)}) %collective-permute-start) | collective-permute-done | bytes 524320 | tf_op jit(solution)/shard_map/ppermute | solution.py:35
  16.1 0.0 collective-permute-start.1
  16.1 8.6 %collective-permute-done.1 = f32[1024,128]{1,0:T(8,128)S(1)} collective-permute-done((f32[1024,128]{1,0:T(8,128)S(1)}, f32[1024,128]{1,0:T(8,128)S(1)}, u32[]{:S(2)}, u32[]{:S(2)}) %collective-permute-start.1) | collective-permute-done | bytes 524320 | tf_op jit(solution)/shard_map/ppermute | solution.py:35
  24.7 0.0 collective-permute-start.2
  24.7 0.0 all-gather.2.cloned.1.call-update
  24.8 0.0 reduce-scatter.2.cloned.1.call-start
  24.8 8.5 %collective-permute-done.2 = f32[1024,128]{1,0:T(8,128)S(1)} collective-permute-done((f32[1024,128]{1,0:T(8,128)S(1)}, f32[1024,128]{1,0:T(8,128)S(1)}, u32[]{:S(2)}, u32[]{:S(2)}) %collective-permute-start.2) | collective-permute-done | bytes 524320 | tf_op jit(solution)/shard_map/ppermute | solution.py:35
  33.3 0.9 constant_dynamic-update-slice_fusion.7
  34.3 0.9 constant_dynamic-update-slice_fusion.6
  35.1 0.9 constant_dynamic-update-slice_fusion.5
  36.0 1.9 %constant_dynamic-update-slice_fusion.4 = f32[1024,1024]{1,0:T(8,128)} fusion(f32[1024,1024]{1,0:T(8,128)} %constant_dynamic-update-slice_fusion.5, f32[1024,128]{1,0:T(8,128)} %param.3), kind=kLoop, calls=%fused_computation.15 | loop fusion | bytes 1048576
  37.9 0.9 constant_dynamic-update-slice_fusion.3
  38.8 0.9 constant_dynamic-update-slice_fusion.2
  39.6 0.9 constant_dynamic-update-slice_fusion.1
  40.5 0.0 copy-done
  40.5 0.0 copy-start.1
  40.5 0.9 constant_dynamic-update-slice_fusion
  41.4 7.1 %all-gather.2.cloned.1.call-done = f32[512,512]{1,0:T(8,128)} async-done(((f32[256,512]{1,0:T(8,128)}), f32[512,512]{1,0:T(8,128)}) %all-gather.2.cloned.1.call-update) | async-done | bytes 1048592 | tf_op jit(solution)/shard_map/all_gather | solution.py:41
  48.5 6.6 %fusion = f32[1024,512]{1,0:T(8,128)} fusion(f32[512,512]{1,0:T(8,128)} %all-gather.2.cloned.1.call-done, f32[1024,1024]{1,0:T(8,128)} %constant_dynamic-update-slice_fusion, s32[]{:T(128)S(6)} %select_n.32), kind=kOutput, calls=%fused_computation | convolution fusion | flops 3221225472 | bytes 5242884 | tf_op jit(solution)/shard_map/dot_general | solution.py:39
  55.1 0.0 reduce-scatter.2.cloned.1.call-update
  55.1 0.0 copy-done.1
  55.2 0.3 fusion.5
  55.4 43.5 %reduce-scatter.2.cloned.1.call-done = f32[256,512]{1,0:T(8,128)} async-done(((f32[1024,512]{1,0:T(8,128)}), f32[256,512]{1,0:T(8,128)}) %reduce-scatter.2.cloned.1.call-update) | async-done | bytes 524304 | tf_op jit(solution)/shard_map/reduce_scatter | solution.py:47
  98.9 1.6 %fusion.3 = (f32[512]{0:T(512)S(1)}, f32[256,512]{1,0:T(8,128)S(1)}) fusion(f32[256,512]{1,0:T(8,128)} %reduce-scatter.2.cloned.1.call-done, f32[256,8]{1,0:T(8,128)S(1)} %fusion.5, s32[512]{0:T(512)S(1)} %add_select_fusion), kind=kOutput, calls=%fused_computation.6 | convolution fusion | flops 12979712 | bytes 1060864 | tf_op jit(solution)/shard_map/dot_general | solution.py:22
  100.4 19.7 %psum.7 = f32[512]{0:T(512)S(1)} all-reduce(f32[512]{0:T(512)S(1)} %get-tuple-element.5), channel_id=1, replica_groups=mesh['row'=2,'col'=4,'layer'=4] {'row','layer'}, use_global_device_ids=true, to_apply=%region_2.3 | all-reduce | flops 512 | bytes 4096 | tf_op jit(solution)/shard_map/psum | solution.py:51
  120.1 1.9 %divide_multiply_fusion = f32[256,512]{1,0:T(8,128)} fusion(f32[512]{0:T(512)S(1)} %psum.7, f32[256,512]{1,0:T(8,128)} %reduce-scatter.2.cloned.1.call-done, f32[256,512]{1,0:T(8,128)S(1)} %get-tuple-element.6), kind=kLoop, calls=%fused_computation.2 | loop fusion | flops 524288 | bytes 1574912 | tf_op jit(solution)/shard_map/mul | solution.py:52
  (2 shorter events, 0.0 us)
Async XLA Ops:
  6.5 34.0 %copy-start = (f32[1024,128]{1,0:T(8,128)S(1)}, f32[1024,128]{1,0:T(8,128)}, u32[]{:S(2)}) copy-start(f32[1024,128]{1,0:T(8,128)} %param.3) | copy-start | bytes 1572868
  6.5 41.9 %all-gather.2.cloned.1.call-start = ((), (), s32[]{:S(2)}) async-start(), calls=%async_computation.1 | async-start | bytes 1572864 | tf_op jit(solution)/shard_map/all_gather | solution.py:41
  6.5 9.6 %collective-permute-start = (f32[1024,128]{1,0:T(8,128)}, f32[1024,128]{1,0:T(8,128)S(1)}, u32[]{:S(2)}, u32[]{:S(2)}) collective-permute-start(f32[1024,128]{1,0:T(8,128)} %param.3), channel_id=1, source_target_pairs={{0,4},{4,8},{8,12},{12,0},{1,5},{5,9},{9,13},{13,1},{2,6},{6,10},{... | collective-permute-start | bytes 1572872 | tf_op jit(solution)/shard_map/ppermute | solution.py:35
  16.1 8.6 %collective-permute-start.1 = (f32[1024,128]{1,0:T(8,128)S(1)}, f32[1024,128]{1,0:T(8,128)S(1)}, u32[]{:S(2)}, u32[]{:S(2)}) collective-permute-start(f32[1024,128]{1,0:T(8,128)S(1)} %collective-permute-done), channel_id=1, source_target_pairs={{0,4},{4,8},{8,12},{12,0},{1,5},{5,9},{9,13},{13,1},{2,6},{6,10},{... | collective-permute-start | bytes 1572872 | tf_op jit(solution)/shard_map/ppermute | solution.py:35
  24.7 8.6 %collective-permute-start.2 = (f32[1024,128]{1,0:T(8,128)S(1)}, f32[1024,128]{1,0:T(8,128)S(1)}, u32[]{:S(2)}, u32[]{:S(2)}) collective-permute-start(f32[1024,128]{1,0:T(8,128)S(1)} %collective-permute-done.1), channel_id=1, source_target_pairs={{0,4},{4,8},{8,12},{12,0},{1,5},{5,9},{9,13},{13,1},{2,6},{6,10},{... | collective-permute-start | bytes 1572872 | tf_op jit(solution)/shard_map/ppermute | solution.py:35
  24.8 74.1 %reduce-scatter.2.cloned.1.call-start = ((), (), s32[]{:S(2)}) async-start(), calls=%async_computation.2 | async-start | bytes 2621440 | tf_op jit(solution)/shard_map/reduce_scatter | solution.py:47
  40.5 14.6 %copy-start.1 = (s32[8,8]{1,0:T(8,128)S(1)}, s32[8,8]{1,0:T(8,128)}, u32[]{:S(2)}) copy-start(s32[8,8]{1,0:T(8,128)} %param.5) | copy-start | bytes 772
Sparse Core Ops, SparseCore 0:
  24.9 23.5 all-gather.1
  55.2 43.6 reduce-scatter.1
